TPU v7x, 256 devices: a whole 4x4x8 slice. The times are simulated.
256 devices in a mesh: dp: 8 (over y, core), cent: 32 (over x, z).
Axes of the slice: x: 4, y: 4, z: 8, core: 2. Of those that a mesh axis runs over, the one named last changes fastest.
Arguments:
- passages: bfloat16 [32768, 768], P(('dp', 'cent')), may hold values from -10 to 10
- queries: bfloat16 [1024, 768], P(('dp', 'cent')), may hold values from -10 to 10
- init_centroids: float32 [8192, 768], P('cent'), may hold values from -12 to 12
- pattern: int32 [1024, 4], replicated, may hold values from 0 to 255, all different within a row
- positive_offset: int32 [1024], replicated, may hold values from 0 to 127
Outputs:
- centroids: float32 [8192, 768], P('cent')
- loss: float32 [1024], P(('dp', 'cent'))
Inputs may be any that keep to these rules, and one draw needn't show every extreme that they name: `pattern`: each row names 4 different blocks.
All inputs are finite; a program needn't handle non-finite values.
Results may differ from a plain program's by a relative error of at most 0.0055.
Values may be sent and summed in bfloat16 or wider, within the bound.
A program may use at most 64 MiB of HBM per device.

v0:
```python
import jax
import jax.numpy as jnp
from jax import lax
from jax.sharding import PartitionSpec as P

BLOCK = 128
ITERS = 2
sharpness = 0.05
sharpening_factor = 0.05
prior_weight = 1.0


def merged(value, axis, join):
    pieces = jax.tree.map(lambda part: lax.all_gather(part, axis), value)
    head = jax.tree.map(lambda part: part[0], pieces)
    tail = jax.tree.map(lambda part: part[1:], pieces)
    so_far, _ = lax.scan(lambda so_far, section: (join(so_far, section), None), head, tail)
    return so_far


def combine_query(first, second):
    upper = jnp.maximum(first[0], second[0])
    total = first[1] * jnp.exp(first[0] - upper) + second[1] * jnp.exp(second[0] - upper)
    return (upper, total, first[2] + second[2])


def on_device(passages, queries, init_centroids, pattern, positive_offset):
    gathered = lax.all_gather(passages, "cent", axis=0, tiled=True)
    cluster_means = init_centroids
    for step_index in range(ITERS):
        centers_half = cluster_means.astype(jnp.bfloat16)
        cluster_center_norms = jnp.sum(cluster_means * cluster_means, axis=1)
        unnormalized_log_odds = sharpness * (
            2.0 * jnp.dot(gathered, centers_half.T, preferred_element_type=jnp.float32)
            - cluster_center_norms[None, :]
        )
        row_max = lax.pmax(jnp.max(unnormalized_log_odds, axis=1), "cent")
        weights_exp = jnp.exp(unnormalized_log_odds - row_max[:, None])
        row_total = lax.psum(jnp.sum(weights_exp, axis=1), "cent")
        resp = weights_exp / row_total[:, None]
        numer = lax.dot_general(
            resp.astype(jnp.bfloat16),
            gathered,
            (((0,), (0,)), ((), ())),
            preferred_element_type=jnp.float32,
        )
        counts = jnp.sum(resp, axis=0)
        numer, counts = lax.psum((numer, counts), "dp")
        cluster_means = (numer + prior_weight * cluster_means) / (counts[:, None] + prior_weight)
    query_collection = lax.all_gather(queries, ("dp", "cent"), axis=0, tiled=True)
    local_rows = passages.shape[0]
    linear = lax.axis_index(("dp", "cent"))
    first_row = linear * local_rows
    local_blocks = first_row // BLOCK + jnp.arange(local_rows // BLOCK, dtype=jnp.int32)
    paired_entries = jnp.any(pattern[:, :, None] == local_blocks[None, None, :], axis=1)
    allowed = jnp.repeat(paired_entries, BLOCK, axis=1)
    affinity_matrix = (
        jnp.dot(query_collection, passages.T, preferred_element_type=jnp.float32)
        * sharpening_factor
    )
    target_col = pattern[:, 0] * BLOCK + positive_offset - first_row
    columns = jnp.arange(local_rows, dtype=jnp.int32)
    positive = jnp.sum(
        jnp.where(columns[None, :] == target_col[:, None], affinity_matrix, 0.0), axis=1
    )
    local_max = jnp.max(jnp.where(allowed, affinity_matrix, -1e30), axis=1)
    local_total = jnp.sum(
        jnp.where(allowed, jnp.exp(affinity_matrix - local_max[:, None]), 0.0), axis=1
    )
    query_max, query_total, positive_all = merged(
        (local_max, local_total, positive), ("dp", "cent"), combine_query
    )
    whole_loss = jnp.log(query_total) + query_max - positive_all
    own_count = queries.shape[0]
    own_loss = lax.dynamic_slice_in_dim(whole_loss, linear * own_count, own_count, 0)
    return (cluster_means, own_loss)


def solution(mesh):
    placed = (P(("dp", "cent"), None), P(("dp", "cent"), None), P("cent", None), P(), P())
    return jax.shard_map(
        on_device,
        mesh=mesh,
        in_specs=placed,
        out_specs=(P("cent", None), P(("dp", "cent"))),
        check_vma=False,
    )
```

profile of v0, /device:TPU:2, one launch (start us, length us, event | category | flops | bytes accessed | tf_op | source)
XLA Modules:
  0.0 1376.9 jit_solution(4740807136776224495)
XLA Ops:
  8.7 108.5 %all-gather.18.cloned.1.call-done = bf16[256,4,768]{2,1,0:T(4,128)(2,1)} async-done(((bf16[1,4,768]{2,1,0:T(4,128)(2,1)}), bf16[256,4,768]{2,1,0:T(4,128)(2,1)}) %all-gather.18.cloned.1.call-update) | async-done | bytes 1572880 | tf_op jit(solution)/shard_map/all_gather | solution.py:50
  117.2 2.7 reshape.42
  120.0 2.2 select_reduce_fusion.2
  123.0 1.4 select_reduce_fusion
  125.8 97.7 %all-gather.12.cloned.1.call-done = f32[262144]{0:T(1024)} async-done(((f32[1024]{0:T(1024)}), f32[262144]{0:T(1024)}) %all-gather.12.cloned.1.call-update) | async-done | bytes 1048592 | tf_op jit(solution)/shard_map/all_gather | solution.py:14
  223.4 1.3 slice.37
  224.9 103.3 %all-gather.14.cloned.1.call-done = f32[262144]{0:T(1024)} async-done(((f32[1024]{0:T(1024)}), f32[262144]{0:T(1024)}) %all-gather.14.cloned.1.call-update) | async-done | bytes 1048592 | tf_op jit(solution)/shard_map/all_gather | solution.py:14
  328.2 1.3 slice.38
  329.5 1.1 reshape.39
  330.6 102.2 %all-gather.16.cloned.1.call-done = f32[262144]{0:T(1024)} async-done(((f32[1024]{0:T(1024)}), f32[262144]{0:T(1024)}) %all-gather.16.cloned.1.call-update) | async-done | bytes 1048592 | tf_op jit(solution)/shard_map/all_gather | solution.py:14
  432.8 1.3 slice.39
  434.1 1.1 reshape.40
  435.2 218.6 %while.14 = (s32[]{:T(128)}, f32[1024]{0:T(1024)S(1)}, f32[1024]{0:T(1024)S(1)}, f32[1024]{0:T(1024)S(1)}, f32[255,1024]{1,0:T(8,128)S(1)}, /*index=5*/f32[255,1024]{1,0:T(8,128)}, f32[255,1024]{1,0:T(8,128)}, s32[]{:T(128)}) while((s32[]{:T(128)}, f32[1024]{0:T(1024)S(1)}, f32[1024]{0:T(1024)S(1)}, f32[1024]{0:T(1024)S(1)}, ...), condition=%wide.region_21.22_spmd, body=%wide.region_20.21_spmd.sunk | while | flops 7170 | bytes 61541 | solution.py:17
  484.1 0.8 constant_dynamic-slice_fusion.5
  654.5 6.7 fusion.18
  661.1 130.3 %pmax.14 = f32[4096]{0:T(1024)S(1)} all-reduce(f32[4096]{0:T(1024)S(1)} %get-tuple-element.66), channel_id=1, replica_groups=mesh['dp'=8,'cent'=32] {'cent'}, use_global_device_ids=true, to_apply=%region_2.0 | all-reduce | flops 4096 | bytes 32768 | tf_op jit(solution)/shard_map/pmax | solution.py:37
  791.4 2.8 fusion.5
  794.2 137.7 %psum.42 = f32[4096]{0:T(1024)S(1)} all-reduce(f32[4096]{0:T(1024)S(1)} %fusion.5), channel_id=1, replica_groups=mesh['dp'=8,'cent'=32] {'cent'}, use_global_device_ids=true, to_apply=%region_4.0 | all-reduce | flops 4096 | bytes 32768 | tf_op jit(solution)/shard_map/psum | solution.py:39
  931.8 6.8 fusion.10
  938.7 3.0 fusion.14
  941.7 12.4 psum.44
  954.1 57.1 %all-reduce.3.cloned.1.call-done = f32[256,768]{1,0:T(8,128)} async-done(((f32[256,768]{1,0:T(8,128)}), f32[256,768]{1,0:T(8,128)}) %all-reduce.3.cloned.1.call-update) | async-done | bytes 786448 | tf_op jit(solution)/shard_map/psum | solution.py:48
  1011.3 1.4 multiply_reduce_fusion
  1012.6 6.7 fusion.19
  1019.3 131.0 %pmax.15 = f32[4096]{0:T(1024)S(1)} all-reduce(f32[4096]{0:T(1024)S(1)} %get-tuple-element.68), channel_id=1, replica_groups=mesh['dp'=8,'cent'=32] {'cent'}, use_global_device_ids=true, to_apply=%region_10.0 | all-reduce | flops 4096 | bytes 32768 | tf_op jit(solution)/shard_map/pmax | solution.py:37
  1150.3 2.8 fusion.6
  1153.1 137.9 %psum.45 = f32[4096]{0:T(1024)S(1)} all-reduce(f32[4096]{0:T(1024)S(1)} %fusion.6), channel_id=1, replica_groups=mesh['dp'=8,'cent'=32] {'cent'}, use_global_device_ids=true, to_apply=%region_12.0 | all-reduce | flops 4096 | bytes 32768 | tf_op jit(solution)/shard_map/psum | solution.py:39
  1291.0 6.8 fusion.8
  1297.8 3.0 fusion.12
  1300.8 12.4 psum.47
  1313.2 54.7 %all-reduce.5.cloned.1.call-done = f32[256,768]{1,0:T(8,128)} async-done(((f32[256,768]{1,0:T(8,128)}), f32[256,768]{1,0:T(8,128)}) %all-reduce.5.cloned.1.call-update) | async-done | bytes 786448 | tf_op jit(solution)/shard_map/psum | solution.py:48
  1367.9 2.1 add_divide_fusion
  (1053 shorter events, 212.3 us)
Async XLA Ops:
  7.2 115.8 %copy-start.1 = (s32[1024]{0:T(1024)S(1)}, s32[1024]{0:T(1024)}, u32[]{:S(2)}) copy-start(s32[1024]{0:T(1024)} %param.11) | copy-start | bytes 12292
  7.2 118.5 %copy-start = (f32[256,768]{1,0:T(8,128)S(1)}, f32[256,768]{1,0:T(8,128)}, u32[]{:S(2)}) copy-start(f32[256,768]{1,0:T(8,128)} %param.9) | copy-start | bytes 2359300
  7.2 110.0 %all-gather.18.cloned.1.call-start = ((), (), s32[]{:S(2)}) async-start(), calls=%async_computation.6 | async-start | bytes 1579008 | tf_op jit(solution)/shard_map/all_gather | solution.py:50
  7.9 215.5 %all-gather.12.cloned.1.call-start = ((), (), s32[]{:S(2)}) async-start(), calls=%async_computation.3 | async-start | bytes 1052672 | tf_op jit(solution)/shard_map/all_gather | solution.py:14
  122.2 206.0 %all-gather.14.cloned.1.call-start = ((), (), s32[]{:S(2)}) async-start(), calls=%async_computation.4 | async-start | bytes 1052672 | tf_op jit(solution)/shard_map/all_gather | solution.py:14
  124.4 308.4 %all-gather.16.cloned.1.call-start = ((), (), s32[]{:S(2)}) async-start(), calls=%async_computation.5 | async-start | bytes 1052672 | tf_op jit(solution)/shard_map/all_gather | solution.py:14
  125.0 529.4 %all-gather.10.cloned.1.call-start = ((), (), s32[]{:S(2)}) async-start(), calls=%async_computation | async-start | bytes 6488064 | tf_op jit(solution)/shard_map/all_gather | solution.py:28
  125.6 885.7 %all-reduce.3.cloned.1.call-start = ((), (), s32[]{:S(2)}) async-start(), calls=%async_computation.1 | async-start | bytes 1572864 | tf_op jit(solution)/shard_map/psum | solution.py:48
  224.9 210.3 %slice-start = ((f32[262144]{0:T(1024)}), f32[1024]{0:T(1024)S(1)}, s32[]{:S(2)}) async-start(f32[262144]{0:T(1024)} %all-gather.12.cloned.1.call-done), calls=%async_computation.7 | async-start | bytes 8192 | tf_op jit(solution)/shard_map/slice | solution.py:15
  328.2 107.0 %slice-start.1 = ((f32[262144]{0:T(1024)}), f32[1024]{0:T(1024)S(1)}, s32[]{:S(2)}) async-start(f32[262144]{0:T(1024)} %all-gather.14.cloned.1.call-done), calls=%async_computation.8 | async-start | bytes 8192 | tf_op jit(solution)/shard_map/slice | solution.py:15
  432.8 2.4 slice-start.2
  938.7 429.2 %all-reduce.5.cloned.1.call-start = ((), (), s32[]{:S(2)}) async-start(), calls=%async_computation.2 | async-start | bytes 1572864 | tf_op jit(solution)/shard_map/psum | solution.py:48
Sparse Core Ops, SparseCore 0:
  11.6 105.6 all-gather.17
  122.3 101.0 all-gather.11
  227.2 100.9 all-gather.13
  331.8 100.9 all-gather.15
  435.2 86.4 all-gather.9
  938.8 72.4 all-reduce.2
  1297.9 69.9 all-reduce.4
where the time goes:
time: 1400 us; the launch traced here: 1380 us
  blocking collectives  562 us (40%)
  waiting for transfers between devices  525 us (38%)
  local copies, waits for them, and re-layouts  214 us (15%)
  matrix products  29.1 us (2%)
  other arithmetic  22.3 us (2%)
  between operations  14.2 us (1%)
    all_gather x3, waiting for transfers between devices, merged(): pieces = jax.tree.map(lambda part: lax.all_gather(part, axis), value)  303 us
    psum x2, blocking collectives, on_device(): row_total = lax.psum(jnp.sum(weights_exp, axis=1), 'cent')  276 us
    pmax x2, blocking collectives, on_device(): row_max = lax.pmax(jnp.max(unnormalized_log_odds, axis=1), 'cent')  261 us
    dynamic_slice x510, local copies, waits for them, and re-layouts, merged(): lax.scan(lambda so_far, section: (join(so_far, section), None), head, tail)  205 us
    psum x2, waiting for transfers between devices, on_device(): numer, counts = lax.psum((numer, counts), 'dp')  112 us
    all_gather x1, waiting for transfers between devices, on_device(): lax.all_gather(queries, ('dp', 'cent'), axis=0, tiled=True)  109 us
  transfers between devices with their start and end apart: 7, of which 6 were waited for; matrix products, arithmetic and copies ran while one was open for 16% of the time, Pallas kernels for 0%

commit v1 on v0

--- a/solution.py
+++ b/solution.py
@@ -36,7 +36,9 @@
         )
         row_max = lax.pmax(jnp.max(unnormalized_log_odds, axis=1), "cent")
         weights_exp = jnp.exp(unnormalized_log_odds - row_max[:, None])
-        row_total = lax.psum(jnp.sum(weights_exp, axis=1), "cent")
+        part_2 = jnp.sum(weights_exp, axis=1)
+        parts = lax.all_gather(part_2, "cent")
+        row_total = jnp.sum(parts, axis=0)
         resp = weights_exp / row_total[:, None]
         numer = lax.dot_general(
             resp.astype(jnp.bfloat16),

time: 1400 us -> 1220 us (0.87)
  blocking collectives: 562 us -> 404 us
  waiting for transfers between devices: 525 us -> 507 us
    psum x2 -> x0, blocking collectives: 276 us -> none  [on_device(): row_total = lax.psum(jnp.sum(weights_exp, axis=1), 'cent')]
    all_gather x0 -> x2, blocking collectives: none -> 118 us  [on_device(): parts = lax.all_gather(part_2, 'cent')]
    psum x2, waiting for transfers between devices: 112 us -> 93.9 us  [on_device(): numer, counts = lax.psum((numer, counts), 'dp')]
  transfers between devices with their start and end apart: 7 -> 7, of which waited for: 6 -> 6; matrix products, arithmetic and copies ran while one was open for 16% -> 19% of each run, Pallas kernels for 0% -> 0%
where the time goes in v1:
time: 1220 us; the launch traced here: 1200 us
  waiting for transfers between devices  507 us (42%)
  blocking collectives  404 us (33%)
  local copies, waits for them, and re-layouts  214 us (18%)
  matrix products  29.1 us (2%)
  other arithmetic  22.4 us (2%)
  between operations  14.3 us (1%)
    all_gather x3, waiting for transfers between devices, merged(): pieces = jax.tree.map(lambda part: lax.all_gather(part, axis), value)  303 us
    pmax x2, blocking collectives, on_device(): row_max = lax.pmax(jnp.max(unnormalized_log_odds, axis=1), 'cent')  261 us
    dynamic_slice x510, local copies, waits for them, and re-layouts, merged(): lax.scan(lambda so_far, section: (join(so_far, section), None), head, tail)  205 us
    all_gather x2, blocking collectives, on_device(): parts = lax.all_gather(part_2, 'cent')  118 us
    all_gather x1, waiting for transfers between devices, on_device(): lax.all_gather(queries, ('dp', 'cent'), axis=0, tiled=True)  109 us
    psum x2, waiting for transfers between devices, on_device(): numer, counts = lax.psum((numer, counts), 'dp')  93.9 us
    psum x2, blocking collectives, on_device(): numer, counts = lax.psum((numer, counts), 'dp')  24.9 us
  transfers between devices with their start and end apart: 7, of which 6 were waited for; matrix products, arithmetic and copies ran while one was open for 19% of the time, Pallas kernels for 0%

profile of v1, /device:TPU:2, one launch (start us, length us, event | category | flops | bytes accessed | tf_op | source)
XLA Modules:
  0.0 1201.4 jit_solution(10555574900278775062)
XLA Ops:
  8.7 108.5 %all-gather.20.cloned.1.call-done = bf16[256,4,768]{2,1,0:T(4,128)(2,1)} async-done(((bf16[1,4,768]{2,1,0:T(4,128)(2,1)}), bf16[256,4,768]{2,1,0:T(4,128)(2,1)}) %all-gather.20.cloned.1.call-update) | async-done | bytes 1572880 | tf_op jit(solution)/shard_map/all_gather | solution.py:52
  117.2 2.7 reshape.44
  120.0 2.2 select_reduce_fusion.2
  123.0 1.4 select_reduce_fusion
  125.8 97.7 %all-gather.14.cloned.1.call-done = f32[262144]{0:T(1024)} async-done(((f32[1024]{0:T(1024)}), f32[262144]{0:T(1024)}) %all-gather.14.cloned.1.call-update) | async-done | bytes 1048592 | tf_op jit(solution)/shard_map/all_gather | solution.py:14
  223.4 1.3 slice.37
  224.9 103.3 %all-gather.16.cloned.1.call-done = f32[262144]{0:T(1024)} async-done(((f32[1024]{0:T(1024)}), f32[262144]{0:T(1024)}) %all-gather.16.cloned.1.call-update) | async-done | bytes 1048592 | tf_op jit(solution)/shard_map/all_gather | solution.py:14
  328.2 1.3 slice.38
  329.5 1.1 reshape.41
  330.6 102.2 %all-gather.18.cloned.1.call-done = f32[262144]{0:T(1024)} async-done(((f32[1024]{0:T(1024)}), f32[262144]{0:T(1024)}) %all-gather.18.cloned.1.call-update) | async-done | bytes 1048592 | tf_op jit(solution)/shard_map/all_gather | solution.py:14
  432.8 1.3 slice.39
  434.1 1.1 reshape.42
  435.2 218.6 %while.14 = (s32[]{:T(128)}, f32[1024]{0:T(1024)S(1)}, f32[1024]{0:T(1024)S(1)}, f32[1024]{0:T(1024)S(1)}, f32[255,1024]{1,0:T(8,128)S(1)}, /*index=5*/f32[255,1024]{1,0:T(8,128)}, f32[255,1024]{1,0:T(8,128)}, s32[]{:T(128)}) while((s32[]{:T(128)}, f32[1024]{0:T(1024)S(1)}, f32[1024]{0:T(1024)S(1)}, f32[1024]{0:T(1024)S(1)}, ...), condition=%wide.region_21.22_spmd, body=%wide.region_20.21_spmd.sunk | while | flops 7170 | bytes 61541 | solution.py:17
  484.1 0.8 constant_dynamic-slice_fusion.5
  654.5 6.7 fusion.18
  661.1 130.2 %pmax.14 = f32[4096]{0:T(1024)S(1)} all-reduce(f32[4096]{0:T(1024)S(1)} %get-tuple-element.66), channel_id=1, replica_groups=mesh['dp'=8,'cent'=32] {'cent'}, use_global_device_ids=true, to_apply=%region_2.0 | all-reduce | flops 4096 | bytes 32768 | tf_op jit(solution)/shard_map/pmax | solution.py:37
  791.4 2.8 fusion.5
  794.1 58.7 %all-gather = f32[131072]{0:T(1024)S(1)} all-gather(f32[4096]{0:T(1024)S(1)} %fusion.5), channel_id=2, replica_groups=mesh['dp'=8,'cent'=32] {'cent'}, dimensions={0}, use_global_device_ids=true | all-gather | bytes 540672 | tf_op jit(solution)/shard_map/all_gather | solution.py:40
  853.0 6.8 fusion.10
  859.9 3.0 fusion.14
  862.9 12.4 %psum.29 = f32[256]{0:T(256)S(1)} all-reduce(f32[256]{0:T(256)S(1)} %fusion.14), channel_id=1, replica_groups=mesh['dp'=8,'cent'=32] {'dp'}, use_global_device_ids=true, to_apply=%region_7.0 | all-reduce | flops 256 | bytes 2048 | tf_op jit(solution)/shard_map/psum | solution.py:50
  875.3 48.1 %all-reduce.3.cloned.1.call-done = f32[256,768]{1,0:T(8,128)} async-done(((f32[256,768]{1,0:T(8,128)}), f32[256,768]{1,0:T(8,128)}) %all-reduce.3.cloned.1.call-update) | async-done | bytes 786448 | tf_op jit(solution)/shard_map/psum | solution.py:50
  923.4 1.4 multiply_reduce_fusion
  924.8 6.7 fusion.19
  931.5 131.0 %pmax.15 = f32[4096]{0:T(1024)S(1)} all-reduce(f32[4096]{0:T(1024)S(1)} %get-tuple-element.68), channel_id=1, replica_groups=mesh['dp'=8,'cent'=32] {'cent'}, use_global_device_ids=true, to_apply=%region_10.0 | all-reduce | flops 4096 | bytes 32768 | tf_op jit(solution)/shard_map/pmax | solution.py:37
  1062.5 2.8 fusion.6
  1065.3 58.9 %all-gather.1 = f32[131072]{0:T(1024)S(1)} all-gather(f32[4096]{0:T(1024)S(1)} %fusion.6), channel_id=3, replica_groups=mesh['dp'=8,'cent'=32] {'cent'}, dimensions={0}, use_global_device_ids=true | all-gather | bytes 540672 | tf_op jit(solution)/shard_map/all_gather | solution.py:40
  1124.4 6.8 fusion.8
  1131.2 3.0 fusion.12
  1134.2 12.4 %psum.31 = f32[256]{0:T(256)S(1)} all-reduce(f32[256]{0:T(256)S(1)} %fusion.12), channel_id=1, replica_groups=mesh['dp'=8,'cent'=32] {'dp'}, use_global_device_ids=true, to_apply=%region_15.0 | all-reduce | flops 256 | bytes 2048 | tf_op jit(solution)/shard_map/psum | solution.py:50
  1146.6 45.8 %all-reduce.5.cloned.1.call-done = f32[256,768]{1,0:T(8,128)} async-done(((f32[256,768]{1,0:T(8,128)}), f32[256,768]{1,0:T(8,128)}) %all-reduce.5.cloned.1.call-update) | async-done | bytes 786448 | tf_op jit(solution)/shard_map/psum | solution.py:50
  1192.4 2.1 add_divide_fusion
  (1057 shorter events, 212.6 us)
Async XLA Ops:
  7.2 115.8 %copy-start.1 = (s32[1024]{0:T(1024)S(1)}, s32[1024]{0:T(1024)}, u32[]{:S(2)}) copy-start(s32[1024]{0:T(1024)} %param.11) | copy-start | bytes 12292
  7.2 118.5 %copy-start = (f32[256,768]{1,0:T(8,128)S(1)}, f32[256,768]{1,0:T(8,128)}, u32[]{:S(2)}) copy-start(f32[256,768]{1,0:T(8,128)} %param.9) | copy-start | bytes 2359300
  7.2 110.0 %all-gather.20.cloned.1.call-start = ((), (), s32[]{:S(2)}) async-start(), calls=%async_computation.6 | async-start | bytes 1579008 | tf_op jit(solution)/shard_map/all_gather | solution.py:52
  7.9 215.5 %all-gather.14.cloned.1.call-start = ((), (), s32[]{:S(2)}) async-start(), calls=%async_computation.3 | async-start | bytes 1052672 | tf_op jit(solution)/shard_map/all_gather | solution.py:14
  122.2 206.0 %all-gather.16.cloned.1.call-start = ((), (), s32[]{:S(2)}) async-start(), calls=%async_computation.4 | async-start | bytes 1052672 | tf_op jit(solution)/shard_map/all_gather | solution.py:14
  124.4 308.4 %all-gather.18.cloned.1.call-start = ((), (), s32[]{:S(2)}) async-start(), calls=%async_computation.5 | async-start | bytes 1052672 | tf_op jit(solution)/shard_map/all_gather | solution.py:14
  125.0 529.4 %all-gather.12.cloned.1.call-start = ((), (), s32[]{:S(2)}) async-start(), calls=%async_computation | async-start | bytes 6488064 | tf_op jit(solution)/shard_map/all_gather | solution.py:28
  125.6 797.8 %all-reduce.3.cloned.1.call-start = ((), (), s32[]{:S(2)}) async-start(), calls=%async_computation.1 | async-start | bytes 1572864 | tf_op jit(solution)/shard_map/psum | solution.py:50
  224.9 210.3 %slice-start = ((f32[262144]{0:T(1024)}), f32[1024]{0:T(1024)S(1)}, s32[]{:S(2)}) async-start(f32[262144]{0:T(1024)} %all-gather.14.cloned.1.call-done), calls=%async_computation.7 | async-start | bytes 8192 | tf_op jit(solution)/shard_map/slice | solution.py:15
  328.2 107.0 %slice-start.1 = ((f32[262144]{0:T(1024)}), f32[1024]{0:T(1024)S(1)}, s32[]{:S(2)}) async-start(f32[262144]{0:T(1024)} %all-gather.16.cloned.1.call-done), calls=%async_computation.8 | async-start | bytes 8192 | tf_op jit(solution)/shard_map/slice | solution.py:15
  432.8 2.4 slice-start.2
  859.9 332.5 %all-reduce.5.cloned.1.call-start = ((), (), s32[]{:S(2)}) async-start(), calls=%async_computation.2 | async-start | bytes 1572864 | tf_op jit(solution)/shard_map/psum | solution.py:50
Sparse Core Ops, SparseCore 0:
  11.6 105.6 all-gather.19
  122.3 101.0 all-gather.13
  227.2 100.9 all-gather.15
  331.8 100.9 all-gather.17
  435.2 86.4 all-gather.11
  860.0 63.3 all-reduce.2
  1131.3 61.0 all-reduce.4
